TPU v7x, 512 devices: a whole 4x8x8 slice. The times are simulated.
512 devices in a mesh: section: 32 (over y_hi, z), dp: 16 (over x, y_lo, core).
Axes of the slice: x: 4, y: 8 (y_hi: 4, y_lo: 2; y = y_hi * 2 + y_lo), z: 8, core: 2. Of those that a mesh axis runs over, the one named last changes fastest.
Arguments:
- checkpoints: bfloat16 [32, 3, 64, 1024], P('section', None, None, 'dp'), may hold values from -6 to 6
- gain: float32 [32, 1024], P('section'), may hold values from 0.25 to 1.75
- w_in: bfloat16 [32, 1024, 8192], P('section', None, 'dp'), may hold values from -0.09375 to 0.09375
- w_out: bfloat16 [32, 8192, 1024], P('section', 'dp'), may hold values from -0.0625 to 0.0625
- cotangent: bfloat16 [3, 64, 4096], P(None, None, 'dp'), may hold values from -6 to 6
Outputs:
- grad_in: bfloat16 [32, 1024, 8192], P('section', None, 'dp')
- grad_out: bfloat16 [32, 8192, 1024], P('section', 'dp')
- grad_gain: float32 [32, 1024], P('section', 'dp')
- section_grads: bfloat16 [32, 3, 64, 1024], P('section', None, None, 'dp')
All inputs are finite; a program needn't handle non-finite values.
Results may differ from a plain program's by a relative error of at most 0.04.
Values may be sent and summed in bfloat16 or wider, within the bound.
A program may use at most 64 MiB of HBM per device.

v0:
```python
import jax
import jax.numpy as jnp
from jax import lax
from jax.sharding import PartitionSpec as P


def from_partner(block, axis, apart):
    count = lax.axis_size(axis)
    route = []
    for low in range(count):
        high = low | 1 << apart
        if high != low and high < count:
            route += [(low, high), (high, low)]
    return lax.ppermute(block, axis, route)


def joined_along(parts, dim):
    dims = list(parts.shape[1:])
    dims[dim] *= parts.shape[0]
    return jnp.moveaxis(parts, 0, dim).reshape(dims)


def from_everyone(x, axis):
    size = lax.axis_size(axis)
    return lax.all_to_all(jnp.broadcast_to(x[None], (size, *x.shape)), axis, 0, 0, tiled=True)


def gathered_copies(x, axis, dim):
    return joined_along(from_everyone(x, axis), dim)


def taken_together(x, axis):
    return from_everyone(x, axis).astype(jnp.float32).sum(axis=0)


def shifted(block, axis, distance):
    devices = range(lax.axis_size(axis))
    route = [(i - distance, i) for i in devices if i - distance in devices]
    return lax.ppermute(block, axis, route)


def gelu_tanh(value):
    return jax.nn.gelu(value, approximate=True)


def quarter_sum(values):
    paired = from_partner(values.astype(jnp.bfloat16), "section", 0).astype(values.dtype)
    first = values + paired
    crossed = from_partner(first.astype(jnp.bfloat16), "section", 1).astype(first.dtype)
    return first + crossed


def activations(summed):
    hidden, pull = jax.vjp(gelu_tanh, summed[0])
    hidden_b = hidden.astype(jnp.bfloat16)
    dact = pull(summed[1])[0].astype(jnp.bfloat16)
    return (hidden_b, dact)


def shards(checkpoints, gain, w_in, w_out, cotangent):
    sections = lax.axis_size("section")
    here = lax.axis_index("section")
    layers = sections // 4
    group = here // 4
    micro = checkpoints.shape[1]
    tok_rows = checkpoints.shape[2]
    share = checkpoints.shape[3]
    quarter = share * lax.axis_size("dp")
    width = 4 * quarter
    offset = lax.axis_index("dp") * share
    gain_row = gain[0]
    weight_in = w_in[0]
    weight_out = w_out[0]
    hidden_dev = weight_in.shape[1]
    ticks = micro + layers - 1
    last = group == layers - 1
    saved = gathered_copies(checkpoints[0], "dp", 2)
    x_full = saved.astype(jnp.float32)
    squares = quarter_sum(jnp.sum(x_full * x_full, axis=-1, keepdims=True))
    scale_all = lax.rsqrt(squares / width + 1e-06)
    normed_all = x_full * scale_all
    scaled_all = (normed_all * gain_row).astype(jnp.bfloat16)
    cot_full = gathered_copies(cotangent, "dp", 2)
    cot_start = here % 4 * quarter

    def timing(tick):
        index = tick - (layers - 1 - group)
        active = (index >= 0) & (index < micro)
        return (jnp.clip(index, 0, micro - 1), active)

    def partials(index, grad_b):
        scaled = lax.dynamic_index_in_dim(scaled_all, index, 0, False)
        act_part = jnp.dot(scaled, weight_in, preferred_element_type=jnp.float32)
        dhid_part = jnp.dot(grad_b, weight_out.T, preferred_element_type=jnp.float32)
        return jnp.stack([act_part, dhid_part])

    def no_partials(index, grad_b):
        return jnp.zeros((2, tok_rows, hidden_dev), jnp.float32)

    def finish(index, grad_b, hidden_b, dact, acc_in, acc_out):
        scaled = lax.dynamic_index_in_dim(scaled_all, index, 0, False)
        acc_out = acc_out + jnp.dot(hidden_b.T, grad_b, preferred_element_type=jnp.float32)
        acc_in = acc_in + jnp.dot(scaled.T, dact, preferred_element_type=jnp.float32)
        partial_value = jnp.dot(dact, weight_in.T, preferred_element_type=jnp.float32)
        return (acc_in, acc_out, partial_value)

    def no_finish(index, grad_b, hidden_b, dact, acc_in, acc_out):
        return (acc_in, acc_out, jnp.zeros((tok_rows, quarter), jnp.float32))

    def layer_work(index, active, grad_b, acc_in, acc_out):
        both = lax.cond(active, partials, no_partials, index, grad_b)
        summed = quarter_sum(both)
        hidden_b, dact = activations(summed)
        return lax.cond(active, finish, no_finish, index, grad_b, hidden_b, dact, acc_in, acc_out)

    acc_in0 = jnp.zeros((quarter, hidden_dev), jnp.float32)
    acc_out0 = jnp.zeros((hidden_dev, quarter), jnp.float32)
    outs0 = jnp.zeros((micro, tok_rows, share), jnp.bfloat16)
    cot_quarter = lax.dynamic_slice_in_dim(cot_full, cot_start, quarter, 2)

    def tick_whole(tick, carry):
        incoming, acc_in, acc_out, acc_gain, outs = carry
        index, active = timing(tick)
        grad_b = jnp.where(last, lax.dynamic_index_in_dim(cot_quarter, index, 0, False), incoming)
        acc_in, acc_out, partial_value = layer_work(index, active, grad_b, acc_in, acc_out)
        normed = lax.dynamic_index_in_dim(normed_all, index, 0, False)
        scale = lax.dynamic_index_in_dim(scale_all, index, 0, False)
        dnorm_in = taken_together(partial_value.astype(jnp.bfloat16), "dp").astype(jnp.float32)
        dnorm = dnorm_in * gain_row
        inner = quarter_sum(jnp.sum(dnorm * normed, axis=-1, keepdims=True)) / width
        grad_x = (grad_b.astype(jnp.float32) + scale * (dnorm - normed * inner)).astype(
            jnp.bfloat16
        )
        acc_gain = acc_gain + jnp.where(active, jnp.sum(dnorm_in * normed, axis=0), 0.0)
        mine = lax.dynamic_slice_in_dim(grad_x, offset, share, 1)
        outs = jnp.where(active, lax.dynamic_update_index_in_dim(outs, mine, index, 0), outs)
        incoming = shifted(grad_x, "section", -4)
        return (incoming, acc_in, acc_out, acc_gain, outs)

    start = (
        jnp.zeros((tok_rows, quarter), jnp.bfloat16),
        acc_in0,
        acc_out0,
        jnp.zeros((quarter,), jnp.float32),
        outs0,
    )
    result = lax.fori_loop(0, ticks, tick_whole, start)
    acc_in, acc_out, acc_gain, outs = (result[1], result[2], result[3], result[4])
    gain_share = lax.dynamic_slice_in_dim(acc_gain, offset, share, 0)
    return (
        acc_in[None].astype(jnp.bfloat16),
        acc_out[None].astype(jnp.bfloat16),
        gain_share[None],
        outs[None],
    )


def solution(mesh):
    in_specs = (
        P("section", None, None, "dp"),
        P("section", None),
        P("section", None, "dp"),
        P("section", "dp", None),
        P(None, None, "dp"),
    )
    out_specs = (
        P("section", None, "dp"),
        P("section", "dp", None),
        P("section", "dp"),
        P("section", None, None, "dp"),
    )
    return jax.shard_map(shards, mesh=mesh, in_specs=in_specs, out_specs=out_specs, check_vma=False)
```

profile of v0, /device:TPU:1, one launch (start us, length us, event | category | flops | bytes accessed | tf_op | source)
XLA Modules:
  0.0 897.5 jit_solution(8416146128455072503)
XLA Ops:
  2.2 17.6 %all_to_all.24 = bf16[16,2,6144]{2,1,0:T(2,128)(2,1)S(1)} all-to-all(bf16[16,2,6144]{2,1,0:T(2,128)(2,1)S(1)} %reshape.43), channel_id=1, replica_groups=mesh['section'=32,'dp'=16] {'dp'}, dimensions={0} | all-to-all | bytes 786432 | tf_op jit(solution)/shard_map/all_to_all | solution.py:25
  21.2 4.8 all-to-all-start.1
  31.4 3.7 collective-permute-start.6
  39.8 7.5 all-to-all-done.1
  50.8 842.2 %while.24 = (s32[]{:T(128)}, bf16[64,1024]{1,0:T(8,128)(2,1)S(1)}, f32[1024,512]{1,0:T(8,128)S(1)}, f32[512,1024]{1,0:T(8,128)}, f32[1024]{0:T(1024)S(1)}, /*ind...) while((s32[]{:T(128)}, bf16[64,1024]{1,0:T(8,128)(2,1)S(1)}, ...), condition=%wide.region_9.10_spmd.clone, body=%wide.region_1.9_spmd.clone.sunk | while | flops 340793856 | bytes 27399740 | solution.py:147
  53.8 3.8 collective-permute-done
  57.6 4.3 collective-permute-start.1
  61.8 5.7 collective-permute-done.1
  68.0 31.9 %all_to_all.25 = bf16[16,64,1024]{2,1,0:T(8,128)(2,1)S(1)} all-to-all(bf16[16,64,1024]{2,1,0:T(8,128)(2,1)S(1)} %broadcast_in_dim.113), channel_id=1, replica_groups=mesh['section'=32,'dp'=16] {'dp'}, dimensions={0} | all-to-all | bytes 4194304 | tf_op jit(solution)/shard_map/while/body/eval_jaxpr/all_to_all | solution.py:25
  107.6 3.8 collective-permute-start.3
  117.5 7.6 collective-permute-done.4
  128.9 5.1 collective-permute-done
  134.0 4.5 collective-permute-start.1
  138.5 3.7 collective-permute-done.1
  142.7 33.7 %all_to_all.25 = bf16[16,64,1024]{2,1,0:T(8,128)(2,1)S(1)} all-to-all(bf16[16,64,1024]{2,1,0:T(8,128)(2,1)S(1)} %broadcast_in_dim.113), channel_id=1, replica_groups=mesh['section'=32,'dp'=16] {'dp'}, dimensions={0} | all-to-all | bytes 4194304 | tf_op jit(solution)/shard_map/while/body/eval_jaxpr/all_to_all | solution.py:25
  184.1 4.4 collective-permute-start.3
  194.1 10.5 %collective-permute-done.4 = bf16[64,1024]{1,0:T(8,128)(2,1)S(1)} collective-permute-done((bf16[64,1024]{1,0:T(8,128)(2,1)S(1)}, bf16[64,1024]{1,0:T(8,128)(2,1)S(1)}, u32[]{:S(2)}, u32[]{:S(2)}) %collective-permute-start.4) | collective-permute-done | bytes 131104 | tf_op jit(solution)/shard_map/while/body/eval_jaxpr/ppermute | solution.py:39
  207.9 4.9 collective-permute-done
  212.9 4.6 collective-permute-start.1
  217.5 3.7 collective-permute-done.1
  221.7 34.0 %all_to_all.25 = bf16[16,64,1024]{2,1,0:T(8,128)(2,1)S(1)} all-to-all(bf16[16,64,1024]{2,1,0:T(8,128)(2,1)S(1)} %broadcast_in_dim.113), channel_id=1, replica_groups=mesh['section'=32,'dp'=16] {'dp'}, dimensions={0} | all-to-all | bytes 4194304 | tf_op jit(solution)/shard_map/while/body/eval_jaxpr/all_to_all | solution.py:25
  263.5 4.1 collective-permute-start.3
  273.3 10.3 %collective-permute-done.4 = bf16[64,1024]{1,0:T(8,128)(2,1)S(1)} collective-permute-done((bf16[64,1024]{1,0:T(8,128)(2,1)S(1)}, bf16[64,1024]{1,0:T(8,128)(2,1)S(1)}, u32[]{:S(2)}, u32[]{:S(2)}) %collective-permute-start.4) | collective-permute-done | bytes 131104 | tf_op jit(solution)/shard_map/while/body/eval_jaxpr/ppermute | solution.py:39
  286.6 6.2 collective-permute-done
  292.9 3.6 collective-permute-start.1
  296.5 4.4 collective-permute-done.1
  301.4 34.5 %all_to_all.25 = bf16[16,64,1024]{2,1,0:T(8,128)(2,1)S(1)} all-to-all(bf16[16,64,1024]{2,1,0:T(8,128)(2,1)S(1)} %broadcast_in_dim.113), channel_id=1, replica_groups=mesh['section'=32,'dp'=16] {'dp'}, dimensions={0} | all-to-all | bytes 4194304 | tf_op jit(solution)/shard_map/while/body/eval_jaxpr/all_to_all | solution.py:25
  353.4 10.3 %collective-permute-done.4 = bf16[64,1024]{1,0:T(8,128)(2,1)S(1)} collective-permute-done((bf16[64,1024]{1,0:T(8,128)(2,1)S(1)}, bf16[64,1024]{1,0:T(8,128)(2,1)S(1)}, u32[]{:S(2)}, u32[]{:S(2)}) %collective-permute-start.4) | collective-permute-done | bytes 131104 | tf_op jit(solution)/shard_map/while/body/eval_jaxpr/ppermute | solution.py:39
  367.1 4.9 collective-permute-done
  372.0 4.6 collective-permute-start.1
  376.6 3.7 collective-permute-done.1
  380.8 34.0 %all_to_all.25 = bf16[16,64,1024]{2,1,0:T(8,128)(2,1)S(1)} all-to-all(bf16[16,64,1024]{2,1,0:T(8,128)(2,1)S(1)} %broadcast_in_dim.113), channel_id=1, replica_groups=mesh['section'=32,'dp'=16] {'dp'}, dimensions={0} | all-to-all | bytes 4194304 | tf_op jit(solution)/shard_map/while/body/eval_jaxpr/all_to_all | solution.py:25
  422.6 4.1 collective-permute-start.3
  432.4 10.5 %collective-permute-done.4 = bf16[64,1024]{1,0:T(8,128)(2,1)S(1)} collective-permute-done((bf16[64,1024]{1,0:T(8,128)(2,1)S(1)}, bf16[64,1024]{1,0:T(8,128)(2,1)S(1)}, u32[]{:S(2)}, u32[]{:S(2)}) %collective-permute-start.4) | collective-permute-done | bytes 131104 | tf_op jit(solution)/shard_map/while/body/eval_jaxpr/ppermute | solution.py:39
  446.1 5.0 collective-permute-done
  451.2 4.3 collective-permute-start.1
  455.5 3.7 collective-permute-done.1
  459.7 34.3 %all_to_all.25 = bf16[16,64,1024]{2,1,0:T(8,128)(2,1)S(1)} all-to-all(bf16[16,64,1024]{2,1,0:T(8,128)(2,1)S(1)} %broadcast_in_dim.113), channel_id=1, replica_groups=mesh['section'=32,'dp'=16] {'dp'}, dimensions={0} | all-to-all | bytes 4194304 | tf_op jit(solution)/shard_map/while/body/eval_jaxpr/all_to_all | solution.py:25
  501.7 4.1 collective-permute-start.3
  511.5 10.4 %collective-permute-done.4 = bf16[64,1024]{1,0:T(8,128)(2,1)S(1)} collective-permute-done((bf16[64,1024]{1,0:T(8,128)(2,1)S(1)}, bf16[64,1024]{1,0:T(8,128)(2,1)S(1)}, u32[]{:S(2)}, u32[]{:S(2)}) %collective-permute-start.4) | collective-permute-done | bytes 131104 | tf_op jit(solution)/shard_map/while/body/eval_jaxpr/ppermute | solution.py:39
  525.0 3.6 collective-permute-done
  528.7 4.5 collective-permute-start.1
  537.2 35.9 %all_to_all.25 = bf16[16,64,1024]{2,1,0:T(8,128)(2,1)S(1)} all-to-all(bf16[16,64,1024]{2,1,0:T(8,128)(2,1)S(1)} %broadcast_in_dim.113), channel_id=1, replica_groups=mesh['section'=32,'dp'=16] {'dp'}, dimensions={0} | all-to-all | bytes 4194304 | tf_op jit(solution)/shard_map/while/body/eval_jaxpr/all_to_all | solution.py:25
  580.9 3.8 collective-permute-start.3
  590.7 40.4 %collective-permute-done.4 = bf16[64,1024]{1,0:T(8,128)(2,1)S(1)} collective-permute-done((bf16[64,1024]{1,0:T(8,128)(2,1)S(1)}, bf16[64,1024]{1,0:T(8,128)(2,1)S(1)}, u32[]{:S(2)}, u32[]{:S(2)}) %collective-permute-start.4) | collective-permute-done | bytes 131104 | tf_op jit(solution)/shard_map/while/body/eval_jaxpr/ppermute | solution.py:39
  636.9 5.3 collective-permute-done
  645.6 4.7 collective-permute-done.1
  650.5 5.2 conditional.7
  656.0 35.1 %all_to_all.25 = bf16[16,64,1024]{2,1,0:T(8,128)(2,1)S(1)} all-to-all(bf16[16,64,1024]{2,1,0:T(8,128)(2,1)S(1)} %broadcast_in_dim.113), channel_id=1, replica_groups=mesh['section'=32,'dp'=16] {'dp'}, dimensions={0} | all-to-all | bytes 4194304 | tf_op jit(solution)/shard_map/while/body/eval_jaxpr/all_to_all | solution.py:25
  698.8 4.0 collective-permute-start.3
  708.6 11.4 %collective-permute-done.4 = bf16[64,1024]{1,0:T(8,128)(2,1)S(1)} collective-permute-done((bf16[64,1024]{1,0:T(8,128)(2,1)S(1)}, bf16[64,1024]{1,0:T(8,128)(2,1)S(1)}, u32[]{:S(2)}, u32[]{:S(2)}) %collective-permute-start.4) | collective-permute-done | bytes 131104 | tf_op jit(solution)/shard_map/while/body/eval_jaxpr/ppermute | solution.py:39
  725.9 4.9 collective-permute-done
  730.8 3.8 collective-permute-start.1
  734.6 3.9 collective-permute-done.1
  738.7 5.2 conditional.7
  744.1 35.8 %all_to_all.25 = bf16[16,64,1024]{2,1,0:T(8,128)(2,1)S(1)} all-to-all(bf16[16,64,1024]{2,1,0:T(8,128)(2,1)S(1)} %broadcast_in_dim.113), channel_id=1, replica_groups=mesh['section'=32,'dp'=16] {'dp'}, dimensions={0} | all-to-all | bytes 4194304 | tf_op jit(solution)/shard_map/while/body/eval_jaxpr/all_to_all | solution.py:25
  787.7 3.9 collective-permute-start.3
  797.5 10.1 %collective-permute-done.4 = bf16[64,1024]{1,0:T(8,128)(2,1)S(1)} collective-permute-done((bf16[64,1024]{1,0:T(8,128)(2,1)S(1)}, bf16[64,1024]{1,0:T(8,128)(2,1)S(1)}, u32[]{:S(2)}, u32[]{:S(2)}) %collective-permute-start.4) | collective-permute-done | bytes 131104 | tf_op jit(solution)/shard_map/while/body/eval_jaxpr/ppermute | solution.py:39
  813.5 4.0 collective-permute-done
  817.5 5.5 collective-permute-start.1
  826.7 5.2 conditional.7
  832.2 35.6 %all_to_all.25 = bf16[16,64,1024]{2,1,0:T(8,128)(2,1)S(1)} all-to-all(bf16[16,64,1024]{2,1,0:T(8,128)(2,1)S(1)} %broadcast_in_dim.113), channel_id=1, replica_groups=mesh['section'=32,'dp'=16] {'dp'}, dimensions={0} | all-to-all | bytes 4194304 | tf_op jit(solution)/shard_map/while/body/eval_jaxpr/all_to_all | solution.py:25
  875.5 4.1 collective-permute-start.3
  885.3 7.7 collective-permute-done.4
  (287 shorter events, 239.3 us)
Async XLA Ops:
  0.6 19.2 %copy-start.2 = (bf16[3,64,256]{2,1,0:T(8,128)(2,1)S(1)}, bf16[3,64,256]{2,1,0:T(8,128)(2,1)}, u32[]{:S(2)}) copy-start(bf16[3,64,256]{2,1,0:T(8,128)(2,1)} %param.15) | copy-start | bytes 294916
  21.2 26.2 %all-to-all-start.1 = ((bf16[16,3,64,256]{3,2,1,0:T(8,128)(2,1)}), bf16[16,3,64,256]{3,2,1,0:T(8,128)(2,1)S(1)}, u32[]{:S(2)}, u32[]{:S(2)}) async-start(bf16[16,3,64,256]{3,2,1,0:T(8,128)(2,1)} %broadcast_in_dim.95), calls=%async_computation.1 | async-start | bytes 3145728 | tf_op jit(solution)/shard_map/all_to_all | solution.py:25
  26.7 4.6 collective-permute-start.5
  31.4 6.1 collective-permute-start.6
  35.2 2.3 copy-start.1
  37.5 10.0 %copy-start.3 = (f32[3,64,1]{1,2,0:T(1,128)}, f32[3,64,1]{1,2,0:T(1,128)S(1)}, u32[]{:S(2)}) copy-start(f32[3,64,1]{1,2,0:T(1,128)S(1)} %add_rsqrt_fusion) | copy-start | bytes 2308
  48.3 2.5 copy-start
  51.8 5.7 collective-permute-start
  57.6 9.9 %collective-permute-start.1 = (bf16[2,64,512]{2,1,0:T(8,128)(2,1)S(1)}, bf16[2,64,512]{2,1,0:T(8,128)(2,1)S(1)}, u32[]{:S(2)}, u32[]{:S(2)}) collective-permute-start(bf16[2,64,512]{2,1,0:T(8,128)(2,1)S(1)} %fusion.40), channel_id=1, source_target_pairs={{0,32},{32,0},{16,48},{48,16},{64,96},{96,64},{80,112},{112,80},{1... | collective-permute-start | bytes 393224 | tf_op jit(solution)/shard_map/while/body/eval_jaxpr/ppermute | solution.py:14
  102.1 4.5 collective-permute-start.2
  107.6 5.4 collective-permute-start.3
  114.8 10.3 %collective-permute-start.4 = (bf16[64,1024]{1,0:T(8,128)(2,1)S(1)}, bf16[64,1024]{1,0:T(8,128)(2,1)S(1)}, u32[]{:S(2)}, u32[]{:S(2)}) collective-permute-start(bf16[64,1024]{1,0:T(8,128)(2,1)S(1)} %fusion.44), channel_id=1, source_target_pairs={{64,0},{80,16},{96,32},{112,48},{128,64},{144,80},{160,96},{176,11... | collective-permute-start | bytes 393224 | tf_op jit(solution)/shard_map/while/body/eval_jaxpr/ppermute | solution.py:39
  126.1 7.9 collective-permute-start
  134.0 8.2 collective-permute-start.1
  178.5 4.5 collective-permute-start.2
  184.1 5.5 collective-permute-start.3
  191.4 13.2 %collective-permute-start.4 = (bf16[64,1024]{1,0:T(8,128)(2,1)S(1)}, bf16[64,1024]{1,0:T(8,128)(2,1)S(1)}, u32[]{:S(2)}, u32[]{:S(2)}) collective-permute-start(bf16[64,1024]{1,0:T(8,128)(2,1)S(1)} %fusion.44), channel_id=1, source_target_pairs={{64,0},{80,16},{96,32},{112,48},{128,64},{144,80},{160,96},{176,11... | collective-permute-start | bytes 393224 | tf_op jit(solution)/shard_map/while/body/eval_jaxpr/ppermute | solution.py:39
  205.6 7.3 collective-permute-start
  212.9 8.3 collective-permute-start.1
  257.9 4.5 collective-permute-start.2
  263.5 5.4 collective-permute-start.3
  270.6 13.0 %collective-permute-start.4 = (bf16[64,1024]{1,0:T(8,128)(2,1)S(1)}, bf16[64,1024]{1,0:T(8,128)(2,1)S(1)}, u32[]{:S(2)}, u32[]{:S(2)}) collective-permute-start(bf16[64,1024]{1,0:T(8,128)(2,1)S(1)} %fusion.44), channel_id=1, source_target_pairs={{64,0},{80,16},{96,32},{112,48},{128,64},{144,80},{160,96},{176,11... | collective-permute-start | bytes 393224 | tf_op jit(solution)/shard_map/while/body/eval_jaxpr/ppermute | solution.py:39
  284.6 8.2 collective-permute-start
  292.9 8.0 collective-permute-start.1
  338.0 4.5 collective-permute-start.2
  343.5 5.4 collective-permute-start.3
  350.7 13.0 %collective-permute-start.4 = (bf16[64,1024]{1,0:T(8,128)(2,1)S(1)}, bf16[64,1024]{1,0:T(8,128)(2,1)S(1)}, u32[]{:S(2)}, u32[]{:S(2)}) collective-permute-start(bf16[64,1024]{1,0:T(8,128)(2,1)S(1)} %fusion.44), channel_id=1, source_target_pairs={{64,0},{80,16},{96,32},{112,48},{128,64},{144,80},{160,96},{176,11... | collective-permute-start | bytes 393224 | tf_op jit(solution)/shard_map/while/body/eval_jaxpr/ppermute | solution.py:39
  364.7 7.3 collective-permute-start
  372.0 8.4 collective-permute-start.1
  417.0 4.5 collective-permute-start.2
  422.6 5.4 collective-permute-start.3
  429.7 13.2 %collective-permute-start.4 = (bf16[64,1024]{1,0:T(8,128)(2,1)S(1)}, bf16[64,1024]{1,0:T(8,128)(2,1)S(1)}, u32[]{:S(2)}, u32[]{:S(2)}) collective-permute-start(bf16[64,1024]{1,0:T(8,128)(2,1)S(1)} %fusion.44), channel_id=1, source_target_pairs={{64,0},{80,16},{96,32},{112,48},{128,64},{144,80},{160,96},{176,11... | collective-permute-start | bytes 393224 | tf_op jit(solution)/shard_map/while/body/eval_jaxpr/ppermute | solution.py:39
  443.9 7.2 collective-permute-start
  451.2 8.1 collective-permute-start.1
  496.1 4.5 collective-permute-start.2
  501.7 5.4 collective-permute-start.3
  508.8 13.1 %collective-permute-start.4 = (bf16[64,1024]{1,0:T(8,128)(2,1)S(1)}, bf16[64,1024]{1,0:T(8,128)(2,1)S(1)}, u32[]{:S(2)}, u32[]{:S(2)}) collective-permute-start(bf16[64,1024]{1,0:T(8,128)(2,1)S(1)} %fusion.44), channel_id=1, source_target_pairs={{64,0},{80,16},{96,32},{112,48},{128,64},{144,80},{160,96},{176,11... | collective-permute-start | bytes 393224 | tf_op jit(solution)/shard_map/while/body/eval_jaxpr/ppermute | solution.py:39
  522.9 5.7 collective-permute-start
  528.7 8.1 collective-permute-start.1
  575.3 4.5 collective-permute-start.2
  580.9 5.4 collective-permute-start.3
  588.0 43.1 %collective-permute-start.4 = (bf16[64,1024]{1,0:T(8,128)(2,1)S(1)}, bf16[64,1024]{1,0:T(8,128)(2,1)S(1)}, u32[]{:S(2)}, u32[]{:S(2)}) collective-permute-start(bf16[64,1024]{1,0:T(8,128)(2,1)S(1)} %fusion.44), channel_id=1, source_target_pairs={{64,0},{80,16},{96,32},{112,48},{128,64},{144,80},{160,96},{176,11... | collective-permute-start | bytes 393224 | tf_op jit(solution)/shard_map/while/body/eval_jaxpr/ppermute | solution.py:39
  635.0 7.3 collective-permute-start
  642.3 8.0 collective-permute-start.1
  693.2 4.5 collective-permute-start.2
  698.8 5.4 collective-permute-start.3
  705.9 14.2 %collective-permute-start.4 = (bf16[64,1024]{1,0:T(8,128)(2,1)S(1)}, bf16[64,1024]{1,0:T(8,128)(2,1)S(1)}, u32[]{:S(2)}, u32[]{:S(2)}) collective-permute-start(bf16[64,1024]{1,0:T(8,128)(2,1)S(1)} %fusion.44), channel_id=1, source_target_pairs={{64,0},{80,16},{96,32},{112,48},{128,64},{144,80},{160,96},{176,11... | collective-permute-start | bytes 393224 | tf_op jit(solution)/shard_map/while/body/eval_jaxpr/ppermute | solution.py:39
  724.0 6.8 collective-permute-start
  730.8 7.7 collective-permute-start.1
  782.1 4.5 collective-permute-start.2
  787.7 5.4 collective-permute-start.3
  794.8 12.9 %collective-permute-start.4 = (bf16[64,1024]{1,0:T(8,128)(2,1)S(1)}, bf16[64,1024]{1,0:T(8,128)(2,1)S(1)}, u32[]{:S(2)}, u32[]{:S(2)}) collective-permute-start(bf16[64,1024]{1,0:T(8,128)(2,1)S(1)} %fusion.44), channel_id=1, source_target_pairs={{64,0},{80,16},{96,32},{112,48},{128,64},{144,80},{160,96},{176,11... | collective-permute-start | bytes 393224 | tf_op jit(solution)/shard_map/while/body/eval_jaxpr/ppermute | solution.py:39
  811.6 5.9 collective-permute-start
  817.5 9.0 %collective-permute-start.1 = (bf16[2,64,512]{2,1,0:T(8,128)(2,1)S(1)}, bf16[2,64,512]{2,1,0:T(8,128)(2,1)S(1)}, u32[]{:S(2)}, u32[]{:S(2)}) collective-permute-start(bf16[2,64,512]{2,1,0:T(8,128)(2,1)S(1)} %fusion.40), channel_id=1, source_target_pairs={{0,32},{32,0},{16,48},{48,16},{64,96},{96,64},{80,112},{112,80},{1... | collective-permute-start | bytes 393224 | tf_op jit(solution)/shard_map/while/body/eval_jaxpr/ppermute | solution.py:14
  869.9 4.5 collective-permute-start.2
  875.5 5.4 collective-permute-start.3
  882.6 10.4 %collective-permute-start.4 = (bf16[64,1024]{1,0:T(8,128)(2,1)S(1)}, bf16[64,1024]{1,0:T(8,128)(2,1)S(1)}, u32[]{:S(2)}, u32[]{:S(2)}) collective-permute-start(bf16[64,1024]{1,0:T(8,128)(2,1)S(1)} %fusion.44), channel_id=1, source_target_pairs={{64,0},{80,16},{96,32},{112,48},{128,64},{144,80},{160,96},{176,11... | collective-permute-start | bytes 393224 | tf_op jit(solution)/shard_map/while/body/eval_jaxpr/ppermute | solution.py:39
where the time goes:
time: 904 us; the launch traced here: 897 us
  blocking collectives  363 us (40%)
  waiting for transfers between devices  252 us (28%)
  starting transfers between devices  149 us (16%)
  other arithmetic  82 us (9%)
  local copies, waits for them, and re-layouts  24.7 us (3%)
  matrix products  24.2 us (3%)
    all_to_all x11, blocking collectives, from_everyone(): lax.all_to_all(jnp.broadcast_to(x[None], (size, *x.shape)), axis, 0, 0, t...  363 us
    ppermute x42, starting transfers between devices, from_partner(): return lax.ppermute(block, axis, route)  132 us
    ppermute x10, waiting for transfers between devices, shifted(): return lax.ppermute(block, axis, route)  129 us
    ppermute x42, waiting for transfers between devices, from_partner(): return lax.ppermute(block, axis, route)  115 us
  transfers between devices with their start and end apart: 53, of which 52 were waited for; matrix products, arithmetic and copies ran while one was open for 4% of the time, Pallas kernels for 0%

commit v1 on v0

v1 whole, which is shorter than its diff:
```python
import functools

import jax
import jax.numpy as jnp
from jax import lax
from jax.experimental import pallas as pl
from jax.experimental.pallas import tpu as pltpu
from jax.sharding import PartitionSpec as P

MESH = pl.DeviceIdType.MESH
F32 = jnp.float32
BF16 = jnp.bfloat16
K0 = 0.7978845608028654
K1 = 0.044715


def dot_nn(a, b):
    return lax.dot_general(a, b, (((1,), (0,)), ((), ())), preferred_element_type=F32)


def dot_nt(a, b):
    return lax.dot_general(a, b, (((1,), (1,)), ((), ())), preferred_element_type=F32)


def dot_tn(a, b):
    return lax.dot_general(a, b, (((0,), (0,)), ((), ())), preferred_element_type=F32)


def chain(
    sizes,
    x_ref, cot_ref, gain_ref, win_ref, wout_ref,
    gin_ref, gout_ref, gg_ref, dxo_ref,
    xsib, xs, xg, dy, shin, rs, qs, dxs, dxsib,
    a1s, a1r, a2s, a2r, apart, sqs, act, slope, hid, dact, ub, rb,
    d1s, d1r, d2s, d2r, dpart, ggacc, ggr,
    sem1, semw,
):
    waves, rows, width, quarter, hidden, sections, peers = sizes
    half = rows // 2
    s = lax.axis_index("section")
    d = lax.axis_index("dp")
    layer, j = s // 4, s % 4
    top = sections // 4 - 1
    g, c = d // 2, d % 2
    sib = d + 1 - 2 * c
    near = s + 1 - 2 * (s % 2)
    far = s + 2 - 4 * ((s // 2) % 2)
    below = (s + sections - 4) % sections
    above = (s + 4) % sections

    def at(section, dp):
        return {"section": section, "dp": dp}

    def remote(src, dst, send, recv, section, dp):
        return pltpu.make_async_remote_copy(
            src_ref=src, dst_ref=dst, send_sem=send, recv_sem=recv,
            device_id=at(section, dp), device_id_type=MESH,
        )

    def take(ref, sem):
        pltpu.make_async_copy(ref, ref, sem).wait()

    barrier = pltpu.get_barrier_semaphore()
    for k in range(1, peers):
        pl.semaphore_signal(barrier, inc=1, device_id=at(s, (d + k) % peers), device_id_type=MESH)
    for other in (near, far, below, above):
        pl.semaphore_signal(barrier, inc=1, device_id=at(other, d), device_id_type=MESH)
    pl.semaphore_wait(barrier, peers + 3)

    SX, RX, SC, SP, RP, SG, RG = range(7)
    (S_XG, R_XG, S_A1, R_A1, S_A2, R_A2, S_SH, R_SH, S_DY, R_DY,
     S_D1, R_D1, S_D2, R_D2, S_RS, R_RS) = range(16)

    own_rows = pl.ds(pl.multiple_of(c * half, half), half)
    own_cols = pl.ds(pl.multiple_of(g * 128, 128), 128)

    pair = remote(x_ref, xsib, sem1.at[SX], sem1.at[RX], s, sib)
    pair.start()

    per = width // quarter
    q = d % per
    holds_cot = (layer == top) & (d // per == j)

    def cot_copies(w, start):
        for b in range(2):
            for hf in range(2):
                owner = q * 4 + b * 2 + hf
                src = cot_ref.at[w, pl.ds(hf * half, half), pl.ds(b * 128, 128)]
                dst = shin.at[w]

                @pl.when(owner == d)
                def _():
                    copy = pltpu.make_async_copy(src, dst, semw.at[R_SH, w])
                    if start:
                        copy.start()

                @pl.when(owner != d)
                def _():
                    copy = remote(src, dst, sem1.at[SC], semw.at[R_SH, w], s, owner)
                    if start:
                        copy.start()
                    else:
                        copy.wait_send()

    @pl.when(holds_cot)
    def _():
        for w in range(waves):
            cot_copies(w, True)

    pair.wait_recv()

    def to_everyone(src, buf, send, recv, w):
        dst = buf.at[w, own_rows, own_cols]
        for k in range(1, peers):
            remote(src, dst, semw.at[send, w], semw.at[recv, w], s, (d + k) % peers).start()
        pltpu.make_async_copy(src, dst, semw.at[recv, w]).start()

    def sent_to_everyone(send, w):
        take(rs.at[w, pl.ds(1, peers - 1)], semw.at[send, w])

    @pl.loop(0, waves)
    def _(w):
        xs[w] = x_ref[w] + xsib[w]
        to_everyone(xs.at[w, own_rows], xg, S_XG, R_XG, w)

    gain = gain_ref[...]

    @pl.loop(0, waves)
    def _(w):
        take(xg.at[w], semw.at[R_XG, w])
        xf = xg[w].astype(F32)
        sq = jnp.sum(xf * xf, axis=-1, keepdims=True)
        sq = jnp.broadcast_to(sq, (rows, 128))
        part = dot_nn((xf * gain).astype(BF16), win_ref[...])
        apart[w] = part
        sqs[w] = sq
        a1s[w, :, :hidden] = part.astype(BF16)
        a1s[w, :, hidden:] = sq.astype(BF16)
        remote(a1s.at[w], a1r.at[w], semw.at[S_A1, w], semw.at[R_A1, w], near, d).start()

    @pl.loop(0, waves)
    def _(w):
        take(a1r.at[w], semw.at[R_A1, w])
        part = apart[w] + a1r[w, :, :hidden].astype(F32)
        sq = sqs[w] + a1r[w, :, hidden:].astype(F32)
        apart[w] = part
        sqs[w] = sq
        a2s[w, :, :hidden] = part.astype(BF16)
        a2s[w, :, hidden:] = sq.astype(BF16)
        remote(a2s.at[w], a2r.at[w], semw.at[S_A2, w], semw.at[R_A2, w], far, d).start()

    @pl.loop(0, waves)
    def _(w):
        take(a2r.at[w], semw.at[R_A2, w])
        part = apart[w] + a2r[w, :, :hidden].astype(F32)
        sq = sqs[w] + a2r[w, :, hidden:].astype(F32)
        r = lax.rsqrt(sq / width + 1e-06)
        rb[w] = r
        r1 = r[:, :1]
        a = part * r1
        t = jnp.tanh(K0 * (a + K1 * a * a * a))
        act[w] = a
        hid[w] = (0.5 * a * (1.0 + t)).astype(BF16)
        slope[w] = 0.5 * (1.0 + t) + 0.5 * a * (1.0 - t * t) * (K0 * (1.0 + 3.0 * K1 * a * a))
        ub[w] = (xg[w].astype(F32) * r1 * gain).astype(BF16)

    ggacc[...] = jnp.zeros_like(ggacc)

    @pl.loop(0, waves)
    def _(w):
        take(shin.at[w], semw.at[R_SH, w])
        to_everyone(shin.at[w], dy, S_DY, R_DY, w)

    @pl.loop(0, waves)
    def _(w):
        take(dy.at[w], semw.at[R_DY, w])
        part = dot_nt(dy[w], wout_ref[...])
        dpart[w] = part
        d1s[w] = part.astype(BF16)
        remote(d1s.at[w], d1r.at[w], semw.at[S_D1, w], semw.at[R_D1, w], near, d).start()

    @pl.loop(0, waves)
    def _(w):
        take(d1r.at[w], semw.at[R_D1, w])
        part = dpart[w] + d1r[w].astype(F32)
        dpart[w] = part
        d2s[w] = part.astype(BF16)
        remote(d2s.at[w], d2r.at[w], semw.at[S_D2, w], semw.at[R_D2, w], far, d).start()

    @pl.loop(0, waves)
    def _(w):
        take(d2r.at[w], semw.at[R_D2, w])
        dh = dpart[w] + d2r[w].astype(F32)
        da = (slope[w] * dh).astype(BF16)
        dact[w] = da
        r1 = rb[w, :, :1]
        mean = jnp.sum(da.astype(F32) * act[w], axis=-1, keepdims=True) / width
        p = dot_nt(da, win_ref[...])
        xf = xg[w].astype(F32)
        n = xf * r1
        ggacc[...] += jnp.broadcast_to(jnp.sum(p * n, axis=0, keepdims=True), ggacc.shape)
        qs[w] = ((p * gain - n * mean) * r1).astype(BF16)
        for k in range(1, peers):
            e = (d + k) % peers
            src = qs.at[w, pl.ds(pl.multiple_of(e % 2 * half, half), half),
                        pl.ds(pl.multiple_of(e // 2 * 128, 128), 128)]
            remote(src, rs.at[w, k], semw.at[S_RS, w], semw.at[R_RS, w], s, e).start()
        pltpu.make_async_copy(qs.at[w, own_rows, own_cols], rs.at[w, 0], semw.at[R_RS, w]).start()

    @pl.loop(0, waves)
    def _(w):
        take(rs.at[w], semw.at[R_RS, w])
        total = dy[w, own_rows, own_cols].astype(F32)
        for k in range(peers):
            total = total + rs[w, k].astype(F32)
        dxs[w] = total.astype(BF16)

        @pl.when(layer > 0)
        def _():
            remote(dxs.at[w], shin.at[w], semw.at[S_SH, w], semw.at[R_SH, w], below, d).start()

    share = remote(dxs, dxsib, sem1.at[SP], sem1.at[RP], s, sib)
    share.start()
    for k in range(1, peers):
        e = (d + k) % peers
        src = ggacc.at[:, pl.ds(pl.multiple_of(e // 2 * 128, 128), 128)]
        remote(src, ggr.at[k], sem1.at[SG], sem1.at[RG], s, e).start()
    pltpu.make_async_copy(ggacc.at[:, own_cols], ggr.at[0], sem1.at[RG]).start()

    tokens = waves * rows
    gout_ref[...] = dot_tn(hid[...].reshape(tokens, hidden), dy[...].reshape(tokens, quarter)).astype(BF16)
    gin_ref[...] = dot_tn(ub[...].reshape(tokens, quarter), dact[...].reshape(tokens, hidden)).astype(BF16)

    take(ggr, sem1.at[RG])
    gg = ggr[0]
    for k in range(1, peers):
        gg = gg + ggr[k]
    gg_ref[...] = gg
    share.wait_recv()
    other_rows = pl.ds(pl.multiple_of((1 - c) * half, half), half)
    for w in range(waves):
        dxo_ref[w, own_rows, :] = dxs[w]
        dxo_ref[w, other_rows, :] = dxsib[w]

    pair.wait_send()
    share.wait_send()
    take(ggr.at[pl.ds(1, peers - 1)], sem1.at[SG])

    @pl.when(holds_cot)
    def _():
        for w in range(waves):
            cot_copies(w, False)

    @pl.loop(0, waves)
    def _(w):
        sent_to_everyone(S_XG, w)
        sent_to_everyone(S_DY, w)
        sent_to_everyone(S_RS, w)
        take(a1s.at[w], semw.at[S_A1, w])
        take(a2s.at[w], semw.at[S_A2, w])
        take(d1s.at[w], semw.at[S_D1, w])
        take(d2s.at[w], semw.at[S_D2, w])

        @pl.when(layer > 0)
        def _():
            take(dxs.at[w], semw.at[S_SH, w])


def shards(checkpoints, gain, w_in, w_out, cotangent):
    sections, peers = lax.axis_size("section"), lax.axis_size("dp")
    waves, rows, share = checkpoints.shape[1:]
    quarter = share * peers
    width = 4 * quarter
    hidden = w_in.shape[2]
    half = rows // 2
    odd = lax.axis_index("dp") % 2
    x = checkpoints[0]
    wide = jnp.concatenate([x, x], axis=-1)
    lane = lax.broadcasted_iota(jnp.int32, wide.shape, 2)
    wide = jnp.where(lane // share == odd, wide, jnp.zeros_like(wide))
    vmem = pl.BlockSpec(memory_space=pltpu.VMEM)
    sizes = (waves, rows, width, quarter, hidden, sections, peers)

    def v(shape, kind=BF16):
        return pltpu.VMEM(shape, kind)

    gin, gout, gg, dxo = pl.pallas_call(
        functools.partial(chain, sizes),
        out_shape=(
            jax.ShapeDtypeStruct((quarter, hidden), BF16),
            jax.ShapeDtypeStruct((hidden, quarter), BF16),
            jax.ShapeDtypeStruct((8, 128), F32),
            jax.ShapeDtypeStruct((waves, rows, 128), BF16),
        ),
        in_specs=[vmem] * 5,
        out_specs=(vmem,) * 4,
        scratch_shapes=[
            v((waves, rows, 128)), v((waves, rows, 128)), v((waves, rows, quarter)),
            v((waves, rows, quarter)), v((waves, half, 128)), v((waves, peers, half, 128)),
            v((waves, rows, quarter)), v((waves, half, 128)), v((waves, half, 128)),
            v((waves, rows, hidden + 128)), v((waves, rows, hidden + 128)),
            v((waves, rows, hidden + 128)), v((waves, rows, hidden + 128)),
            v((waves, rows, hidden), F32), v((waves, rows, 128), F32),
            v((waves, rows, hidden), F32), v((waves, rows, hidden), F32),
            v((waves, rows, hidden)), v((waves, rows, hidden)), v((waves, rows, quarter)),
            v((waves, rows, 128), F32),
            v((waves, rows, hidden)), v((waves, rows, hidden)),
            v((waves, rows, hidden)), v((waves, rows, hidden)),
            v((waves, rows, hidden), F32), v((8, quarter), F32), v((peers, 8, 128), F32),
            pltpu.SemaphoreType.DMA((7,)), pltpu.SemaphoreType.DMA((16, waves)),
        ],
        compiler_params=pltpu.CompilerParams(collective_id=0, has_side_effects=True),
        name="chain",
    )(wide, cotangent, gain, w_in[0], w_out[0])
    start = odd * share
    mine = lax.dynamic_slice_in_dim(dxo, start, share, 2)
    gain_share = lax.dynamic_slice_in_dim(gg[:1], start, share, 1)
    return gin[None], gout[None], gain_share, mine[None]


def solution(mesh):
    in_specs = (
        P("section", None, None, "dp"),
        P("section", None),
        P("section", None, "dp"),
        P("section", "dp", None),
        P(None, None, "dp"),
    )
    out_specs = (
        P("section", None, "dp"),
        P("section", "dp", None),
        P("section", "dp"),
        P("section", None, None, "dp"),
    )
    return jax.shard_map(shards, mesh=mesh, in_specs=in_specs, out_specs=out_specs, check_vma=False)
```

time: 904 us -> 267 us (0.30)
  blocking collectives: 363 us -> 0 us
  Pallas kernels: 0 us -> 259 us
  waiting for transfers between devices: 252 us -> 0 us
  starting transfers between devices: 149 us -> 0 us
  other arithmetic: 82 us -> 1.6 us
  matrix products: 24.2 us -> 0 us
  local copies, waits for them, and re-layouts: 24.7 us -> 6.1 us
    all_to_all x11 -> x0, blocking collectives: 363 us -> none  [from_everyone(): lax.all_to_all(jnp.broadcast_to(x[None], (size, *x.shape)), axis, 0, 0, t...]
    pallas_call x0 -> x1, Pallas kernels: none -> 259 us  [shards(): pl.pallas_call(functools.partial(chain, sizes), out_shape=(jax.ShapeDtype...]
    ppermute x52 -> x0, waiting for transfers between devices: 245 us -> none  [the longest x10 129 us: shifted(): return lax.ppermute(block, axis, route)]
    ppermute x52 -> x0, starting transfers between devices: 145 us -> none  [the longest x42 132 us: from_partner(): return lax.ppermute(block, axis, route)]
    convert_element_type x65 -> x0, other arithmetic: 35.9 us -> none  [the longest x21 11.6 us: quarter_sum(): first.astype(jnp.bfloat16)]
    dot_general x15 -> x0, matrix products: 24.2 us -> none  [the longest x3 10.2 us: finish(): jnp.dot(hidden_b.T, grad_b, preferred_element_type=jnp.float32)]
    select_n x20 -> x1, other arithmetic: 23.3 us -> 1.59 us  [shards(): wide = jnp.where(lane // share == odd, wide, jnp.zeros_like(wide))]
    reduce_sum x21 -> x0, other arithmetic: 15.3 us -> none  [the longest x10 11.1 us: tick_whole(): jnp.sum(dnorm_in * normed, axis=0)]
  transfers between devices with their start and end apart: 53 -> 0, of which waited for: 52 -> 0; matrix products, arithmetic and copies ran while one was open for 4% -> 0% of each run, Pallas kernels for 0% -> 0%
where the time goes in v1:
time: 267 us
  Pallas kernels  259 us (97%)
  local copies, waits for them, and re-layouts  6.1 us (2%)
    pallas_call x1, Pallas kernels, shards(): pl.pallas_call(functools.partial(chain, sizes), out_shape=(jax.ShapeDtype...  259 us

profile of v1, /device:TPU:1, one launch (start us, length us, event | category | flops | bytes accessed | tf_op | source)
XLA Modules:
  0.0 267.1 jit_solution(6515447126138545869)
XLA Ops:
  0.7 1.6 fusion.x_ref
  2.3 258.8 %chain.1 = (bf16[1024,512]{1,0:T(8,128)(2,1)}, bf16[512,1024]{1,0:T(8,128)(2,1)}, f32[8,128]{1,0:T(8,128)}, bf16[3,64,128]{2,1,0:T(8,128)(2,1)}) custom-call(bf16[3,64,128]{2,1,0:T(8,128)(2,1)} %fusion.x_ref, bf16[3,64,256]{2,1,0:T(8,128)(2,1)} %cot_ref.1, f32[1,1024]{1,0:T(1,128)} %gain_ref.1, bf16[1024,512]{1,0:T(8,128)(2,1)} %bitcast.7, ...), custom_call_target="tpu_custom_call" | custom-call | tf_op jit(solution)/shard_map/chain/pallas_call | solution.py:287
  261.0 0.7 slice.3
  261.7 0.6 constant_dynamic-slice_fusion
  262.3 1.5 dynamic-slice_bitcast_fusion
  263.8 0.0 copy-start
  263.8 2.4 copy.11
  266.2 0.0 copy-done
  266.2 1.0 copy.12
  (2 shorter events, 0.0 us)
Async XLA Ops:
  263.8 2.4 copy-start

commit v2 on v1

v2 whole, which is shorter than its diff:
```python
import functools

import jax
import jax.numpy as jnp
from jax import lax
from jax.experimental import pallas as pl
from jax.experimental.pallas import tpu as pltpu
from jax.sharding import PartitionSpec as P

MESH = pl.DeviceIdType.MESH
F32 = jnp.float32
BF16 = jnp.bfloat16
K0 = 0.7978845608028654
K1 = 0.044715
SUB = 4
AT_P1, AT_P2, AT_P3 = 1, 3, 5
AT_A, AT_B1, AT_B2, AT_E = 2, 3, 5, 7


def dot_nn(a, b):
    return lax.dot_general(a, b, (((1,), (0,)), ((), ())), preferred_element_type=F32)


def dot_nt(a, b):
    return lax.dot_general(a, b, (((1,), (1,)), ((), ())), preferred_element_type=F32)


def dot_tn(a, b):
    return lax.dot_general(a, b, (((0,), (0,)), ((), ())), preferred_element_type=F32)


def chain(
    sizes,
    x_ref, cot_ref, gain_ref, win_hbm, wout_hbm,
    hid, dact, ub, dy, gg_ref, dxo_ref,
    win_ref, wout_ref,
    xsib, xs, xg, shin, rs, qs, dxs, dxsib,
    a1s, a1r, a2s, a2r, apart, sqs, act, slope, rb,
    d1s, d1r, d2s, d2r, dpart, ggacc, ggr,
    sem1, semw,
):
    waves, rows, width, quarter, hidden, sections, peers = sizes
    half = rows // 2
    s = lax.axis_index("section")
    d = lax.axis_index("dp")
    layer, j = s // 4, s % 4
    top = sections // 4 - 1
    g, c = d // 2, d % 2
    sib = d + 1 - 2 * c
    near = s + 1 - 2 * (s % 2)
    far = s + 2 - 4 * ((s // 2) % 2)
    below = (s + sections - 4) % sections
    above = (s + 4) % sections

    SX, RX, SC, SG, RG, LI, LO = range(7)
    (S_XG, R_XG, S_A1, R_A1, S_A2, R_A2, S_SH, R_SH, S_DY, R_DY,
     S_D1, R_D1, S_D2, R_D2, S_RS, R_RS, S_SP, R_SP) = range(18)

    def at(section, dp):
        return {"section": section, "dp": dp}

    def remote(src, dst, send, recv, section, dp):
        return pltpu.make_async_remote_copy(
            src_ref=src, dst_ref=dst, send_sem=send, recv_sem=recv,
            device_id=at(section, dp), device_id_type=MESH,
        )

    def take(ref, sem):
        pltpu.make_async_copy(ref, ref, sem).wait()

    load_in = pltpu.make_async_copy(win_hbm, win_ref, sem1.at[LI])
    load_out = pltpu.make_async_copy(wout_hbm, wout_ref, sem1.at[LO])
    load_in.start()
    load_out.start()

    barrier = pltpu.get_barrier_semaphore()
    for k in range(1, peers):
        pl.semaphore_signal(barrier, inc=1, device_id=at(s, (d + k) % peers), device_id_type=MESH)
    for other in (near, far, below, above):
        pl.semaphore_signal(barrier, inc=1, device_id=at(other, d), device_id_type=MESH)
    pl.semaphore_wait(barrier, peers + 3)

    own_rows = pl.ds(pl.multiple_of(c * half, half), half)
    other_rows = pl.ds(pl.multiple_of((1 - c) * half, half), half)
    own_cols = pl.ds(pl.multiple_of(g * 128, 128), 128)

    pair = remote(x_ref, xsib, sem1.at[SX], sem1.at[RX], s, sib)
    pair.start()

    per = width // quarter
    q = d % per
    holds_cot = (layer == top) & (d // per == j)

    def cot_copies(w, start):
        for b in range(2):
            for hf in range(2):
                owner = q * 4 + b * 2 + hf
                src = cot_ref.at[w, pl.ds(hf * half, half), pl.ds(b * 128, 128)]
                dst = shin.at[w]

                if start:
                    @pl.when(owner == d)
                    def _():
                        pltpu.make_async_copy(src, dst, semw.at[R_SH, w]).start()

                @pl.when(owner != d)
                def _():
                    copy = remote(src, dst, sem1.at[SC], semw.at[R_SH, w], s, owner)
                    if start:
                        copy.start()
                    else:
                        copy.wait_send()

    @pl.when(holds_cot)
    def _():
        @pl.loop(0, waves)
        def _(w):
            cot_copies(w, True)

    def to_everyone(src, buf, send, recv, w):
        dst = buf.at[w, own_rows, own_cols]
        for k in range(1, peers):
            remote(src, dst, semw.at[send, w], semw.at[recv, w], s, (d + k) % peers).start()
        pltpu.make_async_copy(src, dst, semw.at[recv, w]).start()

    pair.wait_recv()

    @pl.loop(0, waves)
    def _(w):
        xs[w] = x_ref[w] + xsib[w]
        to_everyone(xs.at[w, own_rows], xg, S_XG, R_XG, w)

    ggacc[...] = jnp.zeros_like(ggacc)
    load_in.wait()
    load_out.wait()

    def stage_p1(w):
        take(xg.at[w], semw.at[R_XG, w])
        gain = gain_ref[...]
        xf = xg[w].astype(F32)
        sq = jnp.sum(xf * xf, axis=-1, keepdims=True)
        sq = jnp.broadcast_to(sq, (rows, 128))
        part = dot_nn((xf * gain).astype(BF16), win_ref[...])
        apart[w] = part
        sqs[w] = sq
        a1s[w, :, :hidden] = part.astype(BF16)
        a1s[w, :, hidden:] = sq.astype(BF16)
        remote(a1s.at[w], a1r.at[w], semw.at[S_A1, w], semw.at[R_A1, w], near, d).start()

    def stage_p2(w):
        take(a1r.at[w], semw.at[R_A1, w])
        part = apart[w] + a1r[w, :, :hidden].astype(F32)
        sq = sqs[w] + a1r[w, :, hidden:].astype(F32)
        apart[w] = part
        sqs[w] = sq
        a2s[w, :, :hidden] = part.astype(BF16)
        a2s[w, :, hidden:] = sq.astype(BF16)
        remote(a2s.at[w], a2r.at[w], semw.at[S_A2, w], semw.at[R_A2, w], far, d).start()

    def stage_p3(w):
        take(a2r.at[w], semw.at[R_A2, w])
        gain = gain_ref[...]
        part = apart[w] + a2r[w, :, :hidden].astype(F32)
        sq = sqs[w] + a2r[w, :, hidden:].astype(F32)
        r = lax.rsqrt(sq / width + 1e-06)
        rb[w] = r
        r1 = r[:, :1]
        a = part * r1
        t = jnp.tanh(K0 * (a + K1 * a * a * a))
        act[w] = a
        hid[w] = (0.5 * a * (1.0 + t)).astype(BF16)
        slope[w] = 0.5 * (1.0 + t) + 0.5 * a * (1.0 - t * t) * (K0 * (1.0 + 3.0 * K1 * a * a))
        ub[w] = (xg[w].astype(F32) * r1 * gain).astype(BF16)

    def stage_g(w):
        take(shin.at[w], semw.at[R_SH, w])
        to_everyone(shin.at[w], dy, S_DY, R_DY, w)

    def stage_a(w):
        take(dy.at[w], semw.at[R_DY, w])
        part = dot_nt(dy[w], wout_ref[...])
        dpart[w] = part
        d1s[w] = part.astype(BF16)
        remote(d1s.at[w], d1r.at[w], semw.at[S_D1, w], semw.at[R_D1, w], near, d).start()

    def stage_b1(w):
        take(d1r.at[w], semw.at[R_D1, w])
        part = dpart[w] + d1r[w].astype(F32)
        dpart[w] = part
        d2s[w] = part.astype(BF16)
        remote(d2s.at[w], d2r.at[w], semw.at[S_D2, w], semw.at[R_D2, w], far, d).start()

    def stage_b2(w):
        take(d2r.at[w], semw.at[R_D2, w])
        gain = gain_ref[...]
        dh = dpart[w] + d2r[w].astype(F32)
        da = (slope[w] * dh).astype(BF16)
        dact[w] = da
        r1 = rb[w, :, :1]
        mean = jnp.sum(da.astype(F32) * act[w], axis=-1, keepdims=True) / width
        p = dot_nt(da, win_ref[...])
        n = xg[w].astype(F32) * r1
        qs[w] = ((p * gain - n * mean) * r1).astype(BF16)
        for k in range(1, peers):
            e = (d + k) % peers
            src = qs.at[w, pl.ds(pl.multiple_of(e % 2 * half, half), half),
                        pl.ds(pl.multiple_of(e // 2 * 128, 128), 128)]
            remote(src, rs.at[w, k], semw.at[S_RS, w], semw.at[R_RS, w], s, e).start()
        pltpu.make_async_copy(qs.at[w, own_rows, own_cols], rs.at[w, 0], semw.at[R_RS, w]).start()
        ggacc[...] += jnp.broadcast_to(jnp.sum(p * n, axis=0, keepdims=True), ggacc.shape)

        @pl.when(w == waves - 1)
        def _():
            for k in range(1, peers):
                e = (d + k) % peers
                src = ggacc.at[:, pl.ds(pl.multiple_of(e // 2 * 128, 128), 128)]
                remote(src, ggr.at[k], sem1.at[SG], sem1.at[RG], s, e).start()
            pltpu.make_async_copy(ggacc.at[:, own_cols], ggr.at[0], sem1.at[RG]).start()

    def stage_e(w):
        take(rs.at[w], semw.at[R_RS, w])
        total = dy[w, own_rows, own_cols].astype(F32)
        for k in range(peers):
            total = total + rs[w, k].astype(F32)
        total = total.astype(BF16)
        dxs[w] = total

        @pl.when(layer > 0)
        def _():
            remote(dxs.at[w], shin.at[w], semw.at[S_SH, w], semw.at[R_SH, w], below, d).start()

        remote(dxs.at[w], dxsib.at[w], semw.at[S_SP, w], semw.at[R_SP, w], s, sib).start()
        dxo_ref[w, own_rows, :] = total

    lag = jnp.where(layer == top, 0, waves + AT_P3 + 1)
    steps = waves + AT_E + waves + AT_P3 + 1

    @pl.loop(0, steps)
    def _(t):
        for w, stage in (
            (t - lag, stage_g),
            (t - AT_P2, stage_p2),
            (t - AT_P3, stage_p3),
            (t - AT_A - lag, stage_a),
            (t - AT_B1 - lag, stage_b1),
            (t - AT_B2 - lag, stage_b2),
            (t - AT_E - lag, stage_e),
            (t - AT_P1, stage_p1),
        ):
            pl.when((w >= 0) & (w < waves))(functools.partial(stage, w))

    take(ggr, sem1.at[RG])
    gg = ggr[0]
    for k in range(1, peers):
        gg = gg + ggr[k]
    gg_ref[...] = gg

    pair.wait_send()
    take(ggr.at[pl.ds(1, peers - 1)], sem1.at[SG])

    @pl.when(holds_cot)
    def _():
        @pl.loop(0, waves)
        def _(w):
            cot_copies(w, False)

    @pl.loop(0, waves)
    def _(w):
        take(dxsib.at[w], semw.at[R_SP, w])
        dxo_ref[w, other_rows, :] = dxsib[w]
        for send in (S_XG, S_DY, S_RS):
            take(rs.at[w, pl.ds(1, peers - 1)], semw.at[send, w])
        take(a1s.at[w], semw.at[S_A1, w])
        take(a2s.at[w], semw.at[S_A2, w])
        take(d1s.at[w], semw.at[S_D1, w])
        take(d2s.at[w], semw.at[S_D2, w])
        take(dxs.at[w], semw.at[S_SP, w])

        @pl.when(layer > 0)
        def _():
            take(dxs.at[w], semw.at[S_SH, w])


def weight_grads(share, hid, dact, ub, dy, gg_ref, dxo_ref, gin_ref, gout_ref, gain_ref, mine_ref):
    gout_ref[...] = dot_tn(hid[...], dy[...]).astype(BF16)
    gin_ref[...] = dot_tn(ub[...], dact[...]).astype(BF16)
    odd = lax.axis_index("dp") % 2

    @pl.when(odd == 0)
    def _():
        gain_ref[...] = gg_ref[:1, :share]
        mine_ref[...] = dxo_ref[:, :share]

    @pl.when(odd == 1)
    def _():
        gain_ref[...] = gg_ref[:1, share:]
        mine_ref[...] = dxo_ref[:, share:]


def shards(checkpoints, gain, w_in, w_out, cotangent):
    sections, peers = lax.axis_size("section"), lax.axis_size("dp")
    waves, rows, share = checkpoints.shape[1:]
    tokens = waves * rows
    waves, rows = waves * SUB, rows // SUB
    quarter = share * peers
    width = 4 * quarter
    hidden = w_in.shape[2]
    half = rows // 2
    odd = lax.axis_index("dp") % 2
    x = checkpoints[0].reshape(waves, rows, share)
    wide = jnp.concatenate([x, x], axis=-1)
    lane = lax.broadcasted_iota(jnp.int32, wide.shape, 2)
    wide = jnp.where(lane // share == odd, wide, jnp.zeros_like(wide))
    vmem = pl.BlockSpec(memory_space=pltpu.VMEM)
    anywhere = pl.BlockSpec(memory_space=pl.ANY)
    sizes = (waves, rows, width, quarter, hidden, sections, peers)

    def v(shape, kind=BF16):
        return pltpu.VMEM(shape, kind)

    def o(shape, kind=BF16):
        return jax.ShapeDtypeStruct(shape, kind)

    hid, dact, ub, dy, gg, dxo = pl.pallas_call(
        functools.partial(chain, sizes),
        out_shape=(
            o((waves, rows, hidden)), o((waves, rows, hidden)),
            o((waves, rows, quarter)), o((waves, rows, quarter)),
            o((8, 128), F32), o((waves, rows, 128)),
        ),
        in_specs=[vmem] * 3 + [anywhere] * 2,
        out_specs=(vmem,) * 6,
        scratch_shapes=[
            v((quarter, hidden)), v((hidden, quarter)),
            v((waves, rows, 128)), v((waves, rows, 128)), v((waves, rows, quarter)),
            v((waves, half, 128)), v((waves, peers, half, 128)),
            v((waves, rows, quarter)), v((waves, half, 128)), v((waves, half, 128)),
            v((waves, rows, hidden + 128)), v((waves, rows, hidden + 128)),
            v((waves, rows, hidden + 128)), v((waves, rows, hidden + 128)),
            v((waves, rows, hidden), F32), v((waves, rows, 128), F32),
            v((waves, rows, hidden), F32), v((waves, rows, hidden), F32),
            v((waves, rows, 128), F32),
            v((waves, rows, hidden)), v((waves, rows, hidden)),
            v((waves, rows, hidden)), v((waves, rows, hidden)),
            v((waves, rows, hidden), F32), v((8, quarter), F32), v((peers, 8, 128), F32),
            pltpu.SemaphoreType.DMA((7,)), pltpu.SemaphoreType.DMA((18, waves)),
        ],
        compiler_params=pltpu.CompilerParams(collective_id=0, has_side_effects=True),
        name="chain",
    )(wide, cotangent.reshape(waves, rows, -1), gain, w_in[0], w_out[0])
    gin, gout, gain_share, mine = pl.pallas_call(
        functools.partial(weight_grads, share),
        out_shape=(o((quarter, hidden)), o((hidden, quarter)), o((1, share), F32), o((tokens, share))),
        in_specs=[vmem] * 6,
        out_specs=(vmem,) * 4,
        name="weight_grads",
    )(
        hid.reshape(tokens, hidden), dact.reshape(tokens, hidden),
        ub.reshape(tokens, quarter), dy.reshape(tokens, quarter), gg, dxo.reshape(tokens, 128),
    )
    return gin[None], gout[None], gain_share, mine.reshape(checkpoints.shape)


def solution(mesh):
    in_specs = (
        P("section", None, None, "dp"),
        P("section", None),
        P("section", None, "dp"),
        P("section", "dp", None),
        P(None, None, "dp"),
    )
    out_specs = (
        P("section", None, "dp"),
        P("section", "dp", None),
        P("section", "dp"),
        P("section", None, None, "dp"),
    )
    return jax.shard_map(shards, mesh=mesh, in_specs=in_specs, out_specs=out_specs, check_vma=False)
```

time: 267 us -> 214 us (0.80)
  Pallas kernels: 259 us -> 211 us
  local copies, waits for them, and re-layouts: 6.1 us -> 0 us
    pallas_call x1 -> x2, Pallas kernels: 259 us -> 211 us  [the longest x1 208 us: shards(): pl.pallas_call(functools.partial(chain, sizes), out_shape=(o((waves, rows...]
    unnamed x4 -> x0, local copies, waits for them, and re-layouts: 3.32 us -> none
where the time goes in v2:
time: 214 us; the launch traced here: 213 us
  Pallas kernels  211 us (99%)
    pallas_call x1, Pallas kernels, shards(): pl.pallas_call(functools.partial(chain, sizes), out_shape=(o((waves, rows...  208 us

profile of v2, /device:TPU:1, one launch (start us, length us, event | category | flops | bytes accessed | tf_op | source)
XLA Modules:
  0.0 213.3 jit_solution(12336736039160908396)
XLA Ops:
  0.7 1.6 fusion.x_ref
  2.3 207.6 %chain.1 = (bf16[12,16,512]{2,1,0:T(8,128)(2,1)}, bf16[12,16,512]{2,1,0:T(8,128)(2,1)}, bf16[12,16,1024]{2,1,0:T(8,128)(2,1)}, bf16[12,16,1024]{2,1,0:T(8,128)(2...) custom-call(bf16[12,16,128]{2,1,0:T(8,128)(2,1)} %fusion.x_ref, bf16[12,16,256]{2,1,0:T(8,128)(2,1)} %bitcast.18, ...), custom_call_target="tpu_custom_call" | custom-call | tf_op jit(solution)/shard_map/chain/pallas_call | solution.py:324
  209.8 3.4 %weight_grads.1 = (bf16[1024,512]{1,0:T(8,128)(2,1)}, bf16[512,1024]{1,0:T(8,128)(2,1)}, f32[1,64]{1,0:T(1,128)}, bf16[192,64]{1,0:T(8,128)(2,1)}) custom-call(bf16[192,512]{1,0:T(8,128)(2,1)} %bitcast.16, bf16[192,512]{1,0:T(8,128)(2,1)} %bitcast.17, bf16[192,1024]{1,0:T(8,128)(2,1)} %bitcast.14, bf16[192,1024]{1,0:T(8,128)(2,1)} %bitcast.15, ...), custom_call_target="tpu_custom_call" | custom-call | tf_op jit(solution)/shard_map/weight_grads/pallas_call | solution.py:351
  (2 shorter events, 0.0 us)

commit v3 on v2

--- a/solution.py
+++ b/solution.py
@@ -13,30 +13,30 @@
 K0 = 0.7978845608028654
 K1 = 0.044715
 SUB = 4
-AT_P1, AT_P2, AT_P3 = 1, 3, 5
-AT_A, AT_B1, AT_B2, AT_E = 2, 3, 5, 7
+GRID = 4
+P1, P2, P3 = 1, 5, 11
+A, B1, B2, E = (6, 2), (8, 3), (11, 6), (14, 9)
+LAG = 0
+ORDER = ('P3', 'G', 'P2', 'E', 'B2', 'P1', 'A', 'B1')
+FAR_FIRST = (8, 7, 9, 6, 10, 5, 11, 4, 12, 3, 13, 2, 14, 1, 15)
 
 
 def dot_nn(a, b):
     return lax.dot_general(a, b, (((1,), (0,)), ((), ())), preferred_element_type=F32)
 
 
-def dot_nt(a, b):
-    return lax.dot_general(a, b, (((1,), (1,)), ((), ())), preferred_element_type=F32)
-
-
 def dot_tn(a, b):
     return lax.dot_general(a, b, (((0,), (0,)), ((), ())), preferred_element_type=F32)
 
 
 def chain(
     sizes,
-    x_ref, cot_ref, gain_ref, win_hbm, wout_hbm,
+    x_in, cot_ref, gain_ref, win_hbm, wout_hbm,
     hid, dact, ub, dy, gg_ref, dxo_ref,
-    win_ref, wout_ref,
+    win_ref, wout_ref, win_t, wout_t, x_ref,
     xsib, xs, xg, shin, rs, qs, dxs, dxsib,
     a1s, a1r, a2s, a2r, apart, sqs, act, slope, rb,
-    d1s, d1r, d2s, d2r, dpart, ggacc, ggr,
+    d1s, d1r, d2s, d2r, dpart, ggacc, ggr, zr,
     sem1, semw,
 ):
     waves, rows, width, quarter, hidden, sections, peers = sizes
@@ -45,6 +45,7 @@
     d = lax.axis_index("dp")
     layer, j = s // 4, s % 4
     top = sections // 4 - 1
+    is_top = layer == top
     g, c = d // 2, d % 2
     sib = d + 1 - 2 * c
     near = s + 1 - 2 * (s % 2)
@@ -54,7 +55,7 @@
 
     SX, RX, SC, SG, RG, LI, LO = range(7)
     (S_XG, R_XG, S_A1, R_A1, S_A2, R_A2, S_SH, R_SH, S_DY, R_DY,
-     S_D1, R_D1, S_D2, R_D2, S_RS, R_RS, S_SP, R_SP) = range(18)
+     S_D1, R_D1, S_D2, R_D2, S_RS, R_RS, S_SP, R_SP, S_Z, R_Z) = range(20)
 
     def at(section, dp):
         return {"section": section, "dp": dp}
@@ -73,12 +74,17 @@
     load_in.start()
     load_out.start()
 
+    share = x_in.shape[2]
+    wide = jnp.concatenate([x_in[...], x_in[...]], axis=-1)
+    lane = lax.broadcasted_iota(jnp.int32, wide.shape, 2)
+    x_ref[...] = jnp.where((lane >= share) == (c == 1), wide, jnp.zeros_like(wide))
+
     barrier = pltpu.get_barrier_semaphore()
     for k in range(1, peers):
         pl.semaphore_signal(barrier, inc=1, device_id=at(s, (d + k) % peers), device_id_type=MESH)
-    for other in (near, far, below, above):
+    for other in (near, far, s - j + 3 - j, below, above):
         pl.semaphore_signal(barrier, inc=1, device_id=at(other, d), device_id_type=MESH)
-    pl.semaphore_wait(barrier, peers + 3)
+    pl.semaphore_wait(barrier, peers + 4)
 
     own_rows = pl.ds(pl.multiple_of(c * half, half), half)
     other_rows = pl.ds(pl.multiple_of((1 - c) * half, half), half)
@@ -119,7 +125,7 @@
 
     def to_everyone(src, buf, send, recv, w):
         dst = buf.at[w, own_rows, own_cols]
-        for k in range(1, peers):
+        for k in FAR_FIRST:
             remote(src, dst, semw.at[send, w], semw.at[recv, w], s, (d + k) % peers).start()
         pltpu.make_async_copy(src, dst, semw.at[recv, w]).start()
 
@@ -133,6 +139,8 @@
     ggacc[...] = jnp.zeros_like(ggacc)
     load_in.wait()
     load_out.wait()
+    win_t[...] = win_ref[...].T
+    wout_t[...] = wout_ref[...].T
 
     def stage_p1(w):
         take(xg.at[w], semw.at[R_XG, w])
@@ -178,10 +186,19 @@
 
     def stage_a(w):
         take(dy.at[w], semw.at[R_DY, w])
-        part = dot_nt(dy[w], wout_ref[...])
+        part = dot_nn(dy[w], wout_t[...])
         dpart[w] = part
         d1s[w] = part.astype(BF16)
-        remote(d1s.at[w], d1r.at[w], semw.at[S_D1, w], semw.at[R_D1, w], near, d).start()
+
+        @pl.when(is_top)
+        def _():
+            remote(d1s.at[w], d1r.at[w], semw.at[S_D1, w], semw.at[R_D1, w], near, d).start()
+
+        @pl.when(layer != top)
+        def _():
+            for k in (2, 1, 3):
+                other = s - j + (j + k) % 4
+                remote(d1s.at[w], zr.at[w, k - 1], semw.at[S_Z, w], semw.at[R_Z, w], other, d).start()
 
     def stage_b1(w):
         take(d1r.at[w], semw.at[R_D1, w])
@@ -191,23 +208,32 @@
         remote(d2s.at[w], d2r.at[w], semw.at[S_D2, w], semw.at[R_D2, w], far, d).start()
 
     def stage_b2(w):
-        take(d2r.at[w], semw.at[R_D2, w])
+        @pl.when(is_top)
+        def _():
+            take(d2r.at[w], semw.at[R_D2, w])
+            dpart[w] = dpart[w] + d2r[w].astype(F32)
+
+        @pl.when(layer != top)
+        def _():
+            take(zr.at[w], semw.at[R_Z, w])
+            dpart[w] = dpart[w] + zr[w, 0].astype(F32) + zr[w, 1].astype(F32) + zr[w, 2].astype(F32)
+
         gain = gain_ref[...]
-        dh = dpart[w] + d2r[w].astype(F32)
+        dh = dpart[w]
         da = (slope[w] * dh).astype(BF16)
         dact[w] = da
         r1 = rb[w, :, :1]
         mean = jnp.sum(da.astype(F32) * act[w], axis=-1, keepdims=True) / width
-        p = dot_nt(da, win_ref[...])
+        p = dot_nn(da, win_t[...])
         n = xg[w].astype(F32) * r1
         qs[w] = ((p * gain - n * mean) * r1).astype(BF16)
-        for k in range(1, peers):
+        for k in FAR_FIRST:
             e = (d + k) % peers
             src = qs.at[w, pl.ds(pl.multiple_of(e % 2 * half, half), half),
                         pl.ds(pl.multiple_of(e // 2 * 128, 128), 128)]
             remote(src, rs.at[w, k], semw.at[S_RS, w], semw.at[R_RS, w], s, e).start()
         pltpu.make_async_copy(qs.at[w, own_rows, own_cols], rs.at[w, 0], semw.at[R_RS, w]).start()
-        ggacc[...] += jnp.broadcast_to(jnp.sum(p * n, axis=0, keepdims=True), ggacc.shape)
+        ggacc[...] += jnp.sum((p * n).reshape(rows // 8, 8, quarter), axis=0)
 
         @pl.when(w == waves - 1)
         def _():
@@ -232,22 +258,26 @@
         remote(dxs.at[w], dxsib.at[w], semw.at[S_SP, w], semw.at[R_SP, w], s, sib).start()
         dxo_ref[w, own_rows, :] = total
 
-    lag = jnp.where(layer == top, 0, waves + AT_P3 + 1)
-    steps = waves + AT_E + waves + AT_P3 + 1
+    base = jnp.where(is_top, LAG, waves + P3 + 1)
+    steps = waves + max(LAG + E[0], waves + P3 + 1 + E[1])
+
+    def chain_at(pair):
+        return base + jnp.where(is_top, pair[0], pair[1])
+
+    stages = dict(
+        G=(base, stage_g), A=(chain_at(A), stage_a), B1=(chain_at(B1), stage_b1),
+        B2=(chain_at(B2), stage_b2), E=(chain_at(E), stage_e),
+        P1=(P1, stage_p1), P2=(P2, stage_p2), P3=(P3, stage_p3),
+    )
 
     @pl.loop(0, steps)
     def _(t):
-        for w, stage in (
-            (t - lag, stage_g),
-            (t - AT_P2, stage_p2),
-            (t - AT_P3, stage_p3),
-            (t - AT_A - lag, stage_a),
-            (t - AT_B1 - lag, stage_b1),
-            (t - AT_B2 - lag, stage_b2),
-            (t - AT_E - lag, stage_e),
-            (t - AT_P1, stage_p1),
-        ):
-            pl.when((w >= 0) & (w < waves))(functools.partial(stage, w))
+        for start, stage in [stages[name] for name in ORDER]:
+            w = t - start
+            live = (w >= 0) & (w < waves)
+            if stage is stage_b1:
+                live = live & is_top
+            pl.when(live)(functools.partial(stage, w))
 
     take(ggr, sem1.at[RG])
     gg = ggr[0]
@@ -272,8 +302,16 @@
             take(rs.at[w, pl.ds(1, peers - 1)], semw.at[send, w])
         take(a1s.at[w], semw.at[S_A1, w])
         take(a2s.at[w], semw.at[S_A2, w])
-        take(d1s.at[w], semw.at[S_D1, w])
-        take(d2s.at[w], semw.at[S_D2, w])
+
+        @pl.when(is_top)
+        def _():
+            take(d1s.at[w], semw.at[S_D1, w])
+            take(d2s.at[w], semw.at[S_D2, w])
+
+        @pl.when(layer != top)
+        def _():
+            take(zr.at[w], semw.at[S_Z, w])
+
         take(dxs.at[w], semw.at[S_SP, w])
 
         @pl.when(layer > 0)
@@ -285,15 +323,16 @@
     gout_ref[...] = dot_tn(hid[...], dy[...]).astype(BF16)
     gin_ref[...] = dot_tn(ub[...], dact[...]).astype(BF16)
     odd = lax.axis_index("dp") % 2
-
-    @pl.when(odd == 0)
+    first = pl.program_id(0) == 0
+
+    @pl.when(first & (odd == 0))
     def _():
-        gain_ref[...] = gg_ref[:1, :share]
+        gain_ref[...] = jnp.sum(gg_ref[:, :share], axis=0, keepdims=True)
         mine_ref[...] = dxo_ref[:, :share]
 
-    @pl.when(odd == 1)
+    @pl.when(first & (odd == 1))
     def _():
-        gain_ref[...] = gg_ref[:1, share:]
+        gain_ref[...] = jnp.sum(gg_ref[:, share:], axis=0, keepdims=True)
         mine_ref[...] = dxo_ref[:, share:]
 
 
@@ -306,14 +345,13 @@
     width = 4 * quarter
     hidden = w_in.shape[2]
     half = rows // 2
-    odd = lax.axis_index("dp") % 2
     x = checkpoints[0].reshape(waves, rows, share)
-    wide = jnp.concatenate([x, x], axis=-1)
-    lane = lax.broadcasted_iota(jnp.int32, wide.shape, 2)
-    wide = jnp.where(lane // share == odd, wide, jnp.zeros_like(wide))
     vmem = pl.BlockSpec(memory_space=pltpu.VMEM)
     anywhere = pl.BlockSpec(memory_space=pl.ANY)
     sizes = (waves, rows, width, quarter, hidden, sections, peers)
+
+    def whole(*shape):
+        return pl.BlockSpec(shape, lambda i: (0, 0))
 
     def v(shape, kind=BF16):
         return pltpu.VMEM(shape, kind)
@@ -331,7 +369,8 @@
         in_specs=[vmem] * 3 + [anywhere] * 2,
         out_specs=(vmem,) * 6,
         scratch_shapes=[
-            v((quarter, hidden)), v((hidden, quarter)),
+            v((quarter, hidden)), v((hidden, quarter)), v((hidden, quarter)), v((quarter, hidden)),
+            v((waves, rows, 128)),
             v((waves, rows, 128)), v((waves, rows, 128)), v((waves, rows, quarter)),
             v((waves, half, 128)), v((waves, peers, half, 128)),
             v((waves, rows, quarter)), v((waves, half, 128)), v((waves, half, 128)),
@@ -343,16 +382,26 @@
             v((waves, rows, hidden)), v((waves, rows, hidden)),
             v((waves, rows, hidden)), v((waves, rows, hidden)),
             v((waves, rows, hidden), F32), v((8, quarter), F32), v((peers, 8, 128), F32),
-            pltpu.SemaphoreType.DMA((7,)), pltpu.SemaphoreType.DMA((18, waves)),
+            v((waves, 3, rows, hidden)),
+            pltpu.SemaphoreType.DMA((7,)), pltpu.SemaphoreType.DMA((20, waves)),
         ],
         compiler_params=pltpu.CompilerParams(collective_id=0, has_side_effects=True),
         name="chain",
-    )(wide, cotangent.reshape(waves, rows, -1), gain, w_in[0], w_out[0])
+    )(x, cotangent.reshape(waves, rows, -1), gain, w_in[0], w_out[0])
     gin, gout, gain_share, mine = pl.pallas_call(
         functools.partial(weight_grads, share),
         out_shape=(o((quarter, hidden)), o((hidden, quarter)), o((1, share), F32), o((tokens, share))),
-        in_specs=[vmem] * 6,
-        out_specs=(vmem,) * 4,
+        grid=(GRID,),
+        in_specs=[
+            pl.BlockSpec((tokens, hidden // GRID), lambda i: (0, i)), whole(tokens, hidden),
+            pl.BlockSpec((tokens, quarter // GRID), lambda i: (0, i)), whole(tokens, quarter),
+            whole(8, 128), whole(tokens, 128),
+        ],
+        out_specs=(
+            pl.BlockSpec((quarter // GRID, hidden), lambda i: (i, 0)),
+            pl.BlockSpec((hidden // GRID, quarter), lambda i: (i, 0)),
+            whole(1, share), whole(tokens, share),
+        ),
         name="weight_grads",
     )(
         hid.reshape(tokens, hidden), dact.reshape(tokens, hidden),

time: 214 us -> 190 us (0.89)
  Pallas kernels: 211 us -> 189 us
    pallas_call x1, Pallas kernels: 208 us -> 185 us  [shards(): pl.pallas_call(functools.partial(chain, sizes), out_shape=(o((waves, rows...]
where the time goes in v3:
time: 190 us
  Pallas kernels  189 us (99%)
    pallas_call x1, Pallas kernels, shards(): pl.pallas_call(functools.partial(chain, sizes), out_shape=(o((waves, rows...  185 us
    pallas_call x1, Pallas kernels, shards(): pl.pallas_call(functools.partial(weight_grads, share), out_shape=(o((quar...  4.45 us

profile of v3, /device:TPU:1, one launch (start us, length us, event | category | flops | bytes accessed | tf_op | source)
XLA Modules:
  0.0 189.6 jit_solution(6380957339216735620)
XLA Ops:
  0.6 184.5 %chain.1 = (bf16[12,16,512]{2,1,0:T(8,128)(2,1)}, bf16[12,16,512]{2,1,0:T(8,128)(2,1)}, bf16[12,16,1024]{2,1,0:T(8,128)(2,1)}, bf16[12,16,1024]{2,1,0:T(8,128)(2...) custom-call(bf16[12,16,64]{2,1,0:T(8,128)(2,1)} %bitcast.20, bf16[12,16,256]{2,1,0:T(8,128)(2,1)} %bitcast.18, ...), custom_call_target="tpu_custom_call" | custom-call | tf_op jit(solution)/shard_map/chain/pallas_call | solution.py:362
  185.2 4.4 %weight_grads.1 = (bf16[1024,512]{1,0:T(8,128)(2,1)}, bf16[512,1024]{1,0:T(8,128)(2,1)}, f32[1,64]{1,0:T(1,128)}, bf16[192,64]{1,0:T(8,128)(2,1)}) custom-call(bf16[192,512]{1,0:T(8,128)(2,1)} %bitcast.16, bf16[192,512]{1,0:T(8,128)(2,1)} %bitcast.17, bf16[192,1024]{1,0:T(8,128)(2,1)} %bitcast.14, bf16[192,1024]{1,0:T(8,128)(2,1)} %bitcast.15, ...), custom_call_target="tpu_custom_call" | custom-call | tf_op jit(solution)/shard_map/weight_grads/pallas_call | solution.py:391

commit v4 on v3

--- a/solution.py
+++ b/solution.py
@@ -13,11 +13,10 @@
 K0 = 0.7978845608028654
 K1 = 0.044715
 SUB = 4
-GRID = 4
-P1, P2, P3 = 1, 5, 11
-A, B1, B2, E = (6, 2), (8, 3), (11, 6), (14, 9)
+P1, P2, P3 = 0, 3, 8
+A, B1, B2, E = (5, 3), (7, 6), (10, 7), (12, 9)
 LAG = 0
-ORDER = ('P3', 'G', 'P2', 'E', 'B2', 'P1', 'A', 'B1')
+ORDER = ('B2', 'A', 'B1', 'G', 'P3', 'P2', 'E', 'P1')
 FAR_FIRST = (8, 7, 9, 6, 10, 5, 11, 4, 12, 3, 13, 2, 14, 1, 15)
 
 
@@ -319,21 +318,40 @@
             take(dxs.at[w], semw.at[S_SH, w])
 
 
-def weight_grads(share, hid, dact, ub, dy, gg_ref, dxo_ref, gin_ref, gout_ref, gain_ref, mine_ref):
-    gout_ref[...] = dot_tn(hid[...], dy[...]).astype(BF16)
-    gin_ref[...] = dot_tn(ub[...], dact[...]).astype(BF16)
+def weight_grads(
+    share, hid, dact, ub, dy, gg_ref, dxo_ref,
+    gin_out, gout_out, gain_ref, mine_ref,
+    gin, gout, sem,
+):
+    tokens = dxo_ref.shape[0] * dxo_ref.shape[1]
     odd = lax.axis_index("dp") % 2
-    first = pl.program_id(0) == 0
-
-    @pl.when(first & (odd == 0))
+
+    @pl.when(odd == 0)
     def _():
         gain_ref[...] = jnp.sum(gg_ref[:, :share], axis=0, keepdims=True)
-        mine_ref[...] = dxo_ref[:, :share]
-
-    @pl.when(first & (odd == 1))
+        mine_ref[...] = dxo_ref[:, :, :share].reshape(tokens, share)
+
+    @pl.when(odd == 1)
     def _():
         gain_ref[...] = jnp.sum(gg_ref[:, share:], axis=0, keepdims=True)
-        mine_ref[...] = dxo_ref[:, share:]
+        mine_ref[...] = dxo_ref[:, :, share:].reshape(tokens, share)
+
+    stores = []
+
+    def product(left, right, result, out, first):
+        part = result.shape[0] // 2
+        for n in range(2):
+            here = pl.ds(n * part, part)
+            lhs = left[:, :, n * part:(n + 1) * part].reshape(tokens, part)
+            rhs = right[...].reshape(tokens, right.shape[2])
+            result[here, :] = dot_tn(lhs, rhs).astype(BF16)
+            stores.append(pltpu.make_async_copy(result.at[here], out.at[here], sem.at[first + n]))
+            stores[-1].start()
+
+    product(hid, dy, gout, gout_out, 0)
+    product(ub, dact, gin, gin_out, 2)
+    for store in stores:
+        store.wait()
 
 
 def shards(checkpoints, gain, w_in, w_out, cotangent):
@@ -350,9 +368,6 @@
     anywhere = pl.BlockSpec(memory_space=pl.ANY)
     sizes = (waves, rows, width, quarter, hidden, sections, peers)
 
-    def whole(*shape):
-        return pl.BlockSpec(shape, lambda i: (0, 0))
-
     def v(shape, kind=BF16):
         return pltpu.VMEM(shape, kind)
 
@@ -362,9 +377,9 @@
     hid, dact, ub, dy, gg, dxo = pl.pallas_call(
         functools.partial(chain, sizes),
         out_shape=(
-            o((waves, rows, hidden)), o((waves, rows, hidden)),
-            o((waves, rows, quarter)), o((waves, rows, quarter)),
-            o((8, 128), F32), o((waves, rows, 128)),
+            pltpu.VMEM((waves, rows, hidden), BF16), pltpu.VMEM((waves, rows, hidden), BF16),
+            pltpu.VMEM((waves, rows, quarter), BF16), pltpu.VMEM((waves, rows, quarter), BF16),
+            pltpu.VMEM((8, 128), F32), pltpu.VMEM((waves, rows, 128), BF16),
         ),
         in_specs=[vmem] * 3 + [anywhere] * 2,
         out_specs=(vmem,) * 6,
@@ -391,21 +406,14 @@
     gin, gout, gain_share, mine = pl.pallas_call(
         functools.partial(weight_grads, share),
         out_shape=(o((quarter, hidden)), o((hidden, quarter)), o((1, share), F32), o((tokens, share))),
-        grid=(GRID,),
-        in_specs=[
-            pl.BlockSpec((tokens, hidden // GRID), lambda i: (0, i)), whole(tokens, hidden),
-            pl.BlockSpec((tokens, quarter // GRID), lambda i: (0, i)), whole(tokens, quarter),
-            whole(8, 128), whole(tokens, 128),
+        in_specs=[vmem] * 6,
+        out_specs=(anywhere, anywhere, vmem, vmem),
+        scratch_shapes=[
+            v((quarter, hidden)), v((hidden, quarter)), pltpu.SemaphoreType.DMA((4,)),
         ],
-        out_specs=(
-            pl.BlockSpec((quarter // GRID, hidden), lambda i: (i, 0)),
-            pl.BlockSpec((hidden // GRID, quarter), lambda i: (i, 0)),
-            whole(1, share), whole(tokens, share),
-        ),
         name="weight_grads",
     )(
-        hid.reshape(tokens, hidden), dact.reshape(tokens, hidden),
-        ub.reshape(tokens, quarter), dy.reshape(tokens, quarter), gg, dxo.reshape(tokens, 128),
+        *[pltpu.with_memory_space_constraint(a, pltpu.MemorySpace.VMEM) for a in (hid, dact, ub, dy, gg, dxo)],
     )
     return gin[None], gout[None], gain_share, mine.reshape(checkpoints.shape)
 

time: 190 us -> 185 us (0.974)
  Pallas kernels: 189 us -> 184 us
    pallas_call x1, Pallas kernels: 185 us -> 182 us  [shards(): pl.pallas_call(functools.partial(chain, sizes), out_shape=(pltpu.VMEM((wa...]
    pallas_call x1, Pallas kernels: 4.45 us -> 2.41 us  [shards(): pl.pallas_call(functools.partial(weight_grads, share), out_shape=(o((quar...]
where the time goes in v4:
time: 185 us
  Pallas kernels  184 us (99%)
    pallas_call x1, Pallas kernels, shards(): pl.pallas_call(functools.partial(chain, sizes), out_shape=(pltpu.VMEM((wa...  182 us

profile of v4, /device:TPU:1, one launch (start us, length us, event | category | flops | bytes accessed | tf_op | source)
XLA Modules:
  0.0 184.7 jit_solution(17811772427315577063)
XLA Ops:
  0.6 181.6 %chain.1 = (bf16[12,16,512]{2,1,0:T(8,128)(2,1)S(1)}, bf16[12,16,512]{2,1,0:T(8,128)(2,1)S(1)}, bf16[12,16,1024]{2,1,0:T(8,128)(2,1)S(1)}, bf16[12,16,1024]{2,1,...) custom-call(bf16[12,16,64]{2,1,0:T(8,128)(2,1)} %bitcast.10, bf16[12,16,256]{2,1,0:T(8,128)(2,1)} %bitcast.9, ...), custom_call_target="tpu_custom_call" | custom-call | tf_op jit(solution)/shard_map/chain/pallas_call | solution.py:377
  182.3 2.4 %weight_grads.1 = (bf16[1024,512]{1,0:T(8,128)(2,1)}, bf16[512,1024]{1,0:T(8,128)(2,1)}, f32[1,64]{1,0:T(1,128)}, bf16[192,64]{1,0:T(8,128)(2,1)}) custom-call(bf16[12,16,512]{2,1,0:T(8,128)(2,1)S(1)} %get-tuple-element.14.hid, bf16[12,16,512]{2,1,0:T(8,128)(2,1)S(1)} %get-tuple-element.15.dact, bf16[12,16,1024]{2,1,0:T(8,128)(2,1)S(1)} %get-tuple-element.16.ub, ...), custom_call_target="tpu_custom_call" | custom-call | tf_op jit(solution)/shard_map/weight_grads/pallas_call | solution.py:406

commit v5 on v4

--- a/solution.py
+++ b/solution.py
@@ -195,9 +195,9 @@
 
         @pl.when(layer != top)
         def _():
-            for k in (2, 1, 3):
-                other = s - j + (j + k) % 4
-                remote(d1s.at[w], zr.at[w, k - 1], semw.at[S_Z, w], semw.at[R_Z, w], other, d).start()
+            for to in (3 - 3 * (j // 2), 2 - j // 2, j + 1 - 2 * (j % 2)):
+                slot = (to - j + 3) % 4
+                remote(d1s.at[w], zr.at[w, slot], semw.at[S_Z, w], semw.at[R_Z, w], s - j + to, d).start()
 
     def stage_b1(w):
         take(d1r.at[w], semw.at[R_D1, w])

time: 185 us -> 185 us (level)
  no operation moved by 1% of the time
where the time goes in v5:
time: 185 us
  Pallas kernels  185 us (100%)
    pallas_call x1, Pallas kernels, shards(): pl.pallas_call(functools.partial(chain, sizes), out_shape=(pltpu.VMEM((wa...  182 us

profile of v5, /device:TPU:1, one launch (start us, length us, event | category | flops | bytes accessed | tf_op | source)
XLA Modules:
  0.0 185.2 jit_solution(258942981658366608)
XLA Ops:
  0.6 182.1 %chain.1 = (bf16[12,16,512]{2,1,0:T(8,128)(2,1)S(1)}, bf16[12,16,512]{2,1,0:T(8,128)(2,1)S(1)}, bf16[12,16,1024]{2,1,0:T(8,128)(2,1)S(1)}, bf16[12,16,1024]{2,1,...) custom-call(bf16[12,16,64]{2,1,0:T(8,128)(2,1)} %bitcast.10, bf16[12,16,256]{2,1,0:T(8,128)(2,1)} %bitcast.9, ...), custom_call_target="tpu_custom_call" | custom-call | tf_op jit(solution)/shard_map/chain/pallas_call | solution.py:377
  182.8 2.4 %weight_grads.1 = (bf16[1024,512]{1,0:T(8,128)(2,1)}, bf16[512,1024]{1,0:T(8,128)(2,1)}, f32[1,64]{1,0:T(1,128)}, bf16[192,64]{1,0:T(8,128)(2,1)}) custom-call(bf16[12,16,512]{2,1,0:T(8,128)(2,1)S(1)} %get-tuple-element.14.hid, bf16[12,16,512]{2,1,0:T(8,128)(2,1)S(1)} %get-tuple-element.15.dact, bf16[12,16,1024]{2,1,0:T(8,128)(2,1)S(1)} %get-tuple-element.16.ub, ...), custom_call_target="tpu_custom_call" | custom-call | tf_op jit(solution)/shard_map/weight_grads/pallas_call | solution.py:406
